TPU v7x, 256 devices: a whole 4x4x8 slice. The times are simulated.
256 devices in a mesh: mem: 32 (over z, x), lon: 4 (over y), lat: 2 (over core).
Axes of the slice: x: 4, y: 4, z: 8, core: 2. Of those that a mesh axis runs over, the one named last changes fastest.
Arguments:
- ens_obs: bfloat16 [1024, 8, 16, 128], P('mem', 'lat', 'lon'), may hold values from -16 to 16
- innovation: bfloat16 [8, 16, 128], P('lat', 'lon'), may hold values from -6 to 6
- obs_weight: bfloat16 [8, 16, 128], P('lat', 'lon'), may hold values from 0.5 to 5
- loc_list: int32 [32, 8, 4], P(None, ('lon', 'lat')), may hold values from 0 to 47, as said below
- counts: int32 [32, 8], P('mem', ('lon', 'lat')), may hold values from 1 to 4, as said below
- taper: float32 [32, 8, 4], P('mem', ('lon', 'lat')), may hold values from 0.2 to 1
- state: bfloat16 [1024, 32, 8, 1280], P('mem', None, ('lon', 'lat')), may hold values from -6 to 6
Outputs:
- analysis: bfloat16 [1024, 32, 8, 1280], P('mem', None, ('lon', 'lat'))
Inputs may be any that keep to these rules, and one draw needn't show every extreme that they name: `loc_list`: the 4 entries of a patch name different window blocks; only the first counts entries are used. `counts`: some patch uses all 4 listed blocks in every draw.
All inputs are finite; a program needn't handle non-finite values.
Results may differ from a plain program's by a relative error of at most 0.0068.
Values may be sent and summed in bfloat16 or wider, within the bound.
A program may use at most 64 MiB of HBM per device.

v0:
```python
import jax
import jax.numpy as jnp
from jax import lax
from jax.sharding import PartitionSpec as P

NSI = 2


def padded(block, sides, width):
    for axis, dim in sides:
        count = lax.axis_size(axis)
        forward = [(i, i + 1) for i in range(count - 1)]
        forward.append((count - 1, 0))
        backward = [(target, source) for source, target in forward]
        low = lax.ppermute(
            lax.slice_in_dim(block, block.shape[dim] - width, None, axis=dim), axis, forward
        )
        high = lax.ppermute(lax.slice_in_dim(block, 0, width, axis=dim), axis, backward)
        block = jnp.concatenate([low, block, high], axis=dim)
    return block


def inverse_root(start_low):
    member_total = start_low.shape[0]
    identity = jnp.eye(member_total, dtype=jnp.float32)
    upper_iter = start_low
    lower_iter = start_low
    for sweep_index in range(NSI):
        if sweep_index == 0:
            product = start_low.astype(jnp.float32)
        else:
            product = jnp.dot(lower_iter, upper_iter, preferred_element_type=jnp.float32)
        halfstep = 0.5 * (3.0 * identity - product)
        half_low = halfstep.astype(jnp.bfloat16)
        if sweep_index == NSI - 1:
            return jnp.dot(half_low, lower_iter, preferred_element_type=jnp.float32)
        next_upper = jnp.dot(upper_iter, half_low, preferred_element_type=jnp.float32).astype(
            jnp.bfloat16
        )
        lower_iter = half_low
        upper_iter = next_upper


def weights_from_gram(gram_mat, drive_vec):
    member_total = gram_mat.shape[0]
    divisor = float(member_total - 1)
    identity = jnp.eye(member_total, dtype=jnp.float32)
    a_matrix = identity + gram_mat / divisor
    trace_level = 2.0 * jnp.trace(a_matrix) / member_total
    start_low = lax.optimization_barrier((a_matrix / trace_level).astype(jnp.bfloat16))
    inv_root = (inverse_root(start_low) / jnp.sqrt(trace_level)).astype(jnp.bfloat16)
    inner_vec = jnp.dot(
        inv_root, (drive_vec / divisor).astype(jnp.bfloat16), preferred_element_type=jnp.float32
    )
    mean_weights = jnp.dot(
        inv_root, inner_vec.astype(jnp.bfloat16), preferred_element_type=jnp.float32
    )
    return (inv_root.astype(jnp.float32) + mean_weights[:, None]).astype(jnp.bfloat16)


def on_device(ens_obs, innovation, obs_weight, loc_list, counts, taper, state):
    local_members, band_rows, band_cols, block_len = ens_obs.shape
    group_patches = loc_list.shape[0]
    slot_count = loc_list.shape[2]
    own_count = taper.shape[0]
    state_len = state.shape[3]
    stacked = jnp.concatenate([ens_obs, innovation[None], obs_weight[None]], axis=0)
    framed = padded(stacked, (("lon", 2),), band_cols)
    window = framed.reshape(local_members + 2, band_rows * 3 * band_cols, block_len)
    picked = window[:, loc_list[:, 0, :], :]
    ens_part = picked[:local_members].reshape(local_members, group_patches, slot_count * block_len)
    first_slot = lax.axis_index("mem") * own_count
    own_side = jnp.moveaxis(
        lax.dynamic_slice_in_dim(picked[local_members:], first_slot, own_count, 1), 1, 0
    )
    flat_state = state.reshape(local_members, group_patches, state_len)
    ens_full = lax.all_to_all(ens_part, "mem", split_axis=1, concat_axis=0, tiled=True)

    def patch_weights(inputs):
        patch_index, tapers, live_count, obs_side = inputs
        selected = lax.dynamic_index_in_dim(ens_full, patch_index, 1, keepdims=False)
        live_mask = (jnp.arange(slot_count, dtype=jnp.int32) < live_count).astype(jnp.float32)
        obs_factor = obs_side[1].astype(jnp.float32) * (tapers * live_mask)[:, None]
        weighted = (selected * obs_factor.reshape(-1)).astype(jnp.bfloat16)
        gram_mat = lax.dot_general(
            weighted, selected, (((1,), (1,)), ((), ())), preferred_element_type=jnp.float32
        )
        drive_vec = jnp.dot(weighted, obs_side[0].reshape(-1), preferred_element_type=jnp.float32)
        return weights_from_gram(gram_mat, drive_vec)

    weight_stack = lax.map(
        patch_weights,
        (jnp.arange(own_count, dtype=jnp.int32), taper[:, 0, :], counts[:, 0], own_side),
    )
    state_full = lax.all_to_all(flat_state, "mem", split_axis=1, concat_axis=0, tiled=True)
    analysis_own = jnp.einsum(
        "pkj,kps->jps", weight_stack, state_full, preferred_element_type=jnp.float32
    ).astype(jnp.bfloat16)
    returned = lax.all_to_all(analysis_own, "mem", split_axis=0, concat_axis=1, tiled=True)
    return returned.reshape(local_members, group_patches, 1, state_len)


def solution(mesh):
    return jax.shard_map(
        on_device,
        mesh=mesh,
        in_specs=(
            P("mem", "lat", "lon", None),
            P("lat", "lon", None),
            P("lat", "lon", None),
            P(None, ("lon", "lat"), None),
            P("mem", ("lon", "lat")),
            P("mem", ("lon", "lat"), None),
            P("mem", None, ("lon", "lat"), None),
        ),
        out_specs=P("mem", None, ("lon", "lat"), None),
        check_vma=False,
    )
```

profile of v0, /device:TPU:32, one launch (start us, length us, event | category | flops | bytes accessed | tf_op | source)
XLA Modules:
  0.0 211.7 jit_solution(16215918792205847067)
XLA Ops:
  0.0 1.0 pad_maximum_fusion.1
  1.0 3.1 %collective-permute-start.1 = (bf16[34,4,4,128]{3,2,1,0:T(4,128)(2,1)S(1)}, bf16[34,4,4,128]{3,2,1,0:T(4,128)(2,1)S(1)}, u32[]{:S(2)}, u32[]{:S(2)}) collective-permute-start(bf16[34,4,4,128]{3,2,1,0:T(4,128)(2,1)S(1)} %pad_maximum_fusion.1), channel_id=1, source_target_pairs={{2,0},{4,2},{6,4},{0,6},{3,1},{5,3},{7,5},{1,7},{10,8},{12,10},{14... | collective-permute-start | bytes 417800 | tf_op jit(solution)/shard_map/ppermute | solution.py:18
  4.1 0.0 collective-permute-start
  4.1 0.7 compare_select_fusion
  4.8 0.1 copy.29
  4.9 0.1 reshape.102
  5.0 2.0 collective-permute-done.1
  7.1 3.4 %collective-permute-done = bf16[34,4,4,128]{3,2,1,0:T(4,128)(2,1)S(1)} collective-permute-done((bf16[34,4,4,128]{3,2,1,0:T(4,128)(2,1)S(1)}, bf16[34,4,4,128]{3,2,1,0:T(4,128)(2,1)S(1)}, u32[]{:S(2)}, u32[]{:S(2)}) %collective-permute-start) | collective-permute-done | bytes 139296 | tf_op jit(solution)/shard_map/ppermute | solution.py:15
  10.5 1.2 pad_maximum_fusion
  11.7 0.3 copy.28
  12.0 0.8 gather_fusion
  12.8 0.6 copy.40
  13.4 0.6 slice.22
  14.1 0.4 reshape.115
  14.5 1.5 copy.35
  16.1 11.2 %all-to-all-start = ((bf16[32,32,512]{2,0,1:T(8,128)(2,1)}), bf16[32,32,512]{2,0,1:T(8,128)(2,1)S(1)}, u32[]{:S(2)}, u32[]{:S(2)}) async-start(bf16[32,32,512]{2,0,1:T(8,128)(2,1)} %copy.35), calls=%async_computation | async-start | bytes 2097152 | tf_op jit(solution)/shard_map/all_to_all | solution.py:77
  27.3 4.7 %copy.39 = bf16[32,32,1,1280]{3,0,1,2:T(8,128)(2,1)} copy(bf16[32,32,1,1280]{3,1,2,0:T(8,128)(2,1)} %param.13) | data formatting | bytes 5242880 | tf_op args[6]
  31.9 21.7 %all-to-all-done = bf16[32,32,512]{2,0,1:T(8,128)(2,1)S(1)} async-done(((bf16[32,32,512]{2,0,1:T(8,128)(2,1)}), bf16[32,32,512]{2,0,1:T(8,128)(2,1)S(1)}, u32[]{:S(2)}, u32[]{:S(2)}) %all-to-all-start) | async-done | bytes 1048608 | tf_op jit(solution)/shard_map/all_to_all | solution.py:77
  53.6 0.0 copy-start.1
  53.6 6.3 %all-to-all-start.1 = ((bf16[32,32,1280]{2,0,1:T(8,128)(2,1)}), bf16[32,32,1280]{2,0,1:T(8,128)(2,1)}, u32[]{:S(2)}, u32[]{:S(2)}) async-start(bf16[32,32,1280]{2,0,1:T(8,128)(2,1)} %bitcast.59), calls=%async_computation.1 | async-start | bytes 5242880 | tf_op jit(solution)/shard_map/all_to_all | solution.py:95
  60.6 0.0 copy-done.1
  60.6 0.1 convert_multiply_fusion
  60.7 0.2 multiply_convert_fusion
  60.9 0.4 fusion.32
  61.3 3.8 %select_reduce_fusion = (f32[]{:T(128)}, f32[1024,1024]{1,0:T(8,128)}) fusion(bf16[1024,512]{1,0:T(8,128)(2,1)S(1)} %bitcast.69, bf16[1024,512]{1,0:T(8,128)(2,1)S(1)} %bitcast.67), kind=kOutput, calls=%fused_computation.10 | convolution fusion | flops 1080033280 | bytes 6291460 | tf_op jit(solution)/shard_map/while/body/eval_jaxpr/dot_general | solution.py:85
  65.8 2.8 %divide_convert_fusion.1 = bf16[1024,1024]{1,0:T(8,128)(2,1)S(1)} fusion(f32[1024,1024]{1,0:T(8,128)} %get-tuple-element.16, f32[]{:T(128)S(6)} %div.29), kind=kLoop, calls=%fused_computation.9 | loop fusion | flops 6291456 | bytes 6291460 | tf_op jit(solution)/shard_map/while/body/eval_jaxpr/convert_element_type | solution.py:50
  68.6 0.0 copy-start
  68.6 1.3 copy-done
  69.9 3.7 %fusion.21 = bf16[1024,1024]{1,0:T(8,128)(2,1)} fusion(bf16[1024,1024]{1,0:T(8,128)(2,1)S(1)} %divide_convert_fusion.1), kind=kOutput, calls=%fused_computation.24 | convolution fusion | flops 2153775104 | bytes 4194304 | tf_op jit(solution)/shard_map/while/body/eval_jaxpr/dot_general | solution.py:37
  73.6 7.4 %divide_convert_fusion = bf16[1024,1024]{1,0:T(8,128)(2,1)S(1)} fusion(f32[]{:T(128)S(6)} %sqrt.4, bf16[1024,1024]{1,0:T(8,128)(2,1)} %fusion.21, bf16[1024,1024]{1,0:T(8,128)(2,1)} %copy-done), kind=kOutput, calls=%fused_computation.8 | convolution fusion | flops 4314890240 | bytes 6291460 | tf_op jit(solution)/shard_map/while/body/eval_jaxpr/dot_general | solution.py:36
  81.0 0.6 fusion.33
  81.7 0.6 fusion.34
  82.3 37.0 %all-to-all-done.1 = bf16[32,32,1280]{2,0,1:T(8,128)(2,1)} async-done(((bf16[32,32,1280]{2,0,1:T(8,128)(2,1)}), bf16[32,32,1280]{2,0,1:T(8,128)(2,1)}, u32[]{:S(2)}, u32[]{:S(2)}) %all-to-all-start.1) | async-done | bytes 2621472 | tf_op jit(solution)/shard_map/all_to_all | solution.py:95
  119.3 6.1 %fusion.4 = bf16[1024,1,1280]{2,0,1:T(8,128)(2,1)} fusion(bf16[1024,1280]{1,0:T(8,128)(2,1)} %bitcast.22, bf16[1024,1024]{1,0:T(8,128)(2,1)S(1)} %divide_convert_fusion, f32[1024]{0:T(1024)S(1)} %bitcast.76), kind=kOutput, calls=%fused_computation.14 | convolution fusion | flops 2688811008 | bytes 7344128 | tf_op jit(solution)/shard_map/pkj,kps->jps/dot_general | solution.py:96
  125.4 0.5 broadcast.106
  126.0 4.4 %reduce = bf16[1024,1280]{1,0:T(8,128)(2,1)S(1)} reduce(bf16[1024,1,1280]{2,0,1:T(8,128)(2,1)} %fusion.4, bf16[]{:T(256)} %broadcast.106), dimensions={1}, to_apply=%copy.33.reduce_sub_computation | reduce | bytes 5242882 | tf_op jit(solution)/shard_map/convert_element_type | solution.py:98
  130.4 2.2 %reshape.116 = bf16[32,2,20480]{2,1,0:T(2,128)(2,1)} reshape(bf16[1024,1280]{1,0:T(8,128)(2,1)S(1)} %reduce) | data formatting | bytes 5242880
  132.6 66.1 %all_to_all.45 = bf16[32,2,20480]{2,1,0:T(2,128)(2,1)S(1)} all-to-all(bf16[32,2,20480]{2,1,0:T(2,128)(2,1)} %reshape.116), channel_id=1, replica_groups=mesh['mem'=32,'lon'=4,'lat'=2] {'mem'}, dimensions={0} | all-to-all | bytes 5242880 | tf_op jit(solution)/shard_map/all_to_all | solution.py:99
  198.7 7.2 %reshape.117 = bf16[1024,1,1280]{2,1,0:T(2,128)(2,1)} reshape(bf16[32,2,20480]{2,1,0:T(2,128)(2,1)S(1)} %all_to_all.45) | data formatting | bytes 5242880
  205.9 2.9 %copy.36 = bf16[1024,1,1280]{2,0,1:T(8,128)(2,1)S(1)} copy(bf16[1024,1,1280]{2,1,0:T(2,128)(2,1)} %reshape.117) | data formatting | bytes 5242880
  208.8 2.9 %copy.34 = bf16[32,32,1,1280]{3,1,2,0:T(8,128)(2,1)} copy(bf16[32,32,1,1280]{3,0,1,2:T(8,128)(2,1)S(1)} %bitcast.62) | data formatting | bytes 5242880 | tf_op jit(solution)/shard_map/all_to_all | solution.py:99
  (9 shorter events, 0.1 us)
Async XLA Ops:
  1.0 6.0 %collective-permute-start.1 = (bf16[34,4,4,128]{3,2,1,0:T(4,128)(2,1)S(1)}, bf16[34,4,4,128]{3,2,1,0:T(4,128)(2,1)S(1)}, u32[]{:S(2)}, u32[]{:S(2)}) collective-permute-start(bf16[34,4,4,128]{3,2,1,0:T(4,128)(2,1)S(1)} %pad_maximum_fusion.1), channel_id=1, source_target_pairs={{2,0},{4,2},{6,4},{0,6},{3,1},{5,3},{7,5},{1,7},{10,8},{12,10},{14... | collective-permute-start | bytes 417800 | tf_op jit(solution)/shard_map/ppermute | solution.py:18
  4.1 6.3 %collective-permute-start = (bf16[34,4,4,128]{3,2,1,0:T(4,128)(2,1)S(1)}, bf16[34,4,4,128]{3,2,1,0:T(4,128)(2,1)S(1)}, u32[]{:S(2)}, u32[]{:S(2)}) collective-permute-start(bf16[34,4,4,128]{3,2,1,0:T(4,128)(2,1)S(1)} %pad_maximum_fusion.1), channel_id=1, source_target_pairs={{0,2},{2,4},{4,6},{6,0},{1,3},{3,5},{5,7},{7,1},{8,10},{10,12},{12... | collective-permute-start | bytes 417800 | tf_op jit(solution)/shard_map/ppermute | solution.py:15
  16.1 37.6 %all-to-all-start = ((bf16[32,32,512]{2,0,1:T(8,128)(2,1)}), bf16[32,32,512]{2,0,1:T(8,128)(2,1)S(1)}, u32[]{:S(2)}, u32[]{:S(2)}) async-start(bf16[32,32,512]{2,0,1:T(8,128)(2,1)} %copy.35), calls=%async_computation | async-start | bytes 2097152 | tf_op jit(solution)/shard_map/all_to_all | solution.py:77
  53.6 6.9 %copy-start.1 = (f32[1,1,4]{2,1,0:T(1,128)S(1)}, f32[1,1,4]{2,1,0:T(1,128)}, u32[]{:S(2)}) copy-start(f32[1,1,4]{2,1,0:T(1,128)} %param.12) | copy-start | bytes 52
  53.6 65.7 %all-to-all-start.1 = ((bf16[32,32,1280]{2,0,1:T(8,128)(2,1)}), bf16[32,32,1280]{2,0,1:T(8,128)(2,1)}, u32[]{:S(2)}, u32[]{:S(2)}) async-start(bf16[32,32,1280]{2,0,1:T(8,128)(2,1)} %bitcast.59), calls=%async_computation.1 | async-start | bytes 5242880 | tf_op jit(solution)/shard_map/all_to_all | solution.py:95
  68.6 1.3 copy-start
where the time goes:
time: 212 us
  blocking collectives  66.1 us (31%)
  waiting for transfers between devices  64.1 us (30%)
  local copies, waits for them, and re-layouts  26.3 us (12%)
  matrix products  22.7 us (11%)
  starting transfers between devices  20.6 us (10%)
  other arithmetic  10.5 us (5%)
    all_to_all x1, blocking collectives, on_device(): lax.all_to_all(analysis_own, 'mem', split_axis=0, concat_axis=1, tiled=True)  66.1 us
    all_to_all x1, waiting for transfers between devices, on_device(): lax.all_to_all(flat_state, 'mem', split_axis=1, concat_axis=0, tiled=True)  37 us
    all_to_all x1, waiting for transfers between devices, on_device(): lax.all_to_all(ens_part, 'mem', split_axis=1, concat_axis=0, tiled=True)  21.7 us
    unnamed x8, local copies, waits for them, and re-layouts  18.3 us
    all_to_all x1, starting transfers between devices, on_device(): lax.all_to_all(ens_part, 'mem', split_axis=1, concat_axis=0, tiled=True)  11.2 us
    dot_general x1, matrix products, inverse_root(): return jnp.dot(half_low, lower_iter, preferred_element_type=jnp.float32)  7.36 us
    all_to_all x1, starting transfers between devices, on_device(): lax.all_to_all(flat_state, 'mem', split_axis=1, concat_axis=0, tiled=True)  6.28 us
    dot_general x1, matrix products, on_device(): jnp.einsum('pkj,kps->jps', weight_stack, state_full, preferred_element_ty...  6.13 us
  transfers between devices with their start and end apart: 4, of which 4 were waited for; matrix products, arithmetic and copies ran while one was open for 12% of the time, Pallas kernels for 0%

commit v1 on v0

--- a/solution.py
+++ b/solution.py
@@ -1,9 +1,19 @@
+import functools
 import jax
 import jax.numpy as jnp
 from jax import lax
 from jax.sharding import PartitionSpec as P
 
 NSI = 2
+
+
+def state_the_notes(own_rows, axis_no, out_dim):
+    y_new = lax.axis_size("mem")
+    side_arr = lax.all_to_all(jnp.stack(jnp.split(own_rows, y_new, axis_no), 0), "mem", 0, 0)
+    return jnp.concatenate(side_arr, out_dim)
+
+
+return_all_signs_over_axis = functools.partial(state_the_notes, axis_no=0, out_dim=1)
 
 
 def padded(block, sides, width):
@@ -96,7 +106,7 @@
     analysis_own = jnp.einsum(
         "pkj,kps->jps", weight_stack, state_full, preferred_element_type=jnp.float32
     ).astype(jnp.bfloat16)
-    returned = lax.all_to_all(analysis_own, "mem", split_axis=0, concat_axis=1, tiled=True)
+    returned = return_all_signs_over_axis(analysis_own)
     return returned.reshape(local_members, group_patches, 1, state_len)
 
 

time: 212 us -> 194 us (0.915)
  local copies, waits for them, and re-layouts: 26.3 us -> 13.7 us
  other arithmetic: 10.5 us -> 6.08 us
    unnamed x8 -> x36, local copies, waits for them, and re-layouts: 18.3 us -> 6.23 us
    convert_element_type x1 -> x0, other arithmetic: 4.42 us -> none  [on_device(): analysis_own = jnp.einsum('pkj,kps->jps', weight_stack, state_full, prefe...]
    all_to_all x1 -> x0, local copies, waits for them, and re-layouts: 2.93 us -> none  [on_device(): lax.all_to_all(analysis_own, 'mem', split_axis=0, concat_axis=1, tiled=True)]
    reshape x0 -> x1, local copies, waits for them, and re-layouts: none -> 2.93 us  [state_the_notes(): return jnp.concatenate(side_arr, out_dim)]
  transfers between devices with their start and end apart: 4 -> 4, of which waited for: 4 -> 4; matrix products, arithmetic and copies ran while one was open for 12% -> 13% of each run, Pallas kernels for 0% -> 0%
where the time goes in v1:
time: 194 us
  blocking collectives  65.9 us (34%)
  waiting for transfers between devices  64 us (33%)
  matrix products  21.7 us (11%)
  starting transfers between devices  20.6 us (11%)
  local copies, waits for them, and re-layouts  13.7 us (7%)
  other arithmetic  6.08 us (3%)
    all_to_all x1, blocking collectives, state_the_notes(): lax.all_to_all(jnp.stack(jnp.split(own_rows, y_new, axis_no), 0), 'mem',...  65.9 us
    all_to_all x1, waiting for transfers between devices, on_device(): lax.all_to_all(flat_state, 'mem', split_axis=1, concat_axis=0, tiled=True)  36.8 us
    all_to_all x1, waiting for transfers between devices, on_device(): lax.all_to_all(ens_part, 'mem', split_axis=1, concat_axis=0, tiled=True)  21.7 us
    all_to_all x1, starting transfers between devices, on_device(): lax.all_to_all(ens_part, 'mem', split_axis=1, concat_axis=0, tiled=True)  11.2 us
    dot_general x1, matrix products, inverse_root(): return jnp.dot(half_low, lower_iter, preferred_element_type=jnp.float32)  7.36 us
    all_to_all x1, starting transfers between devices, on_device(): lax.all_to_all(flat_state, 'mem', split_axis=1, concat_axis=0, tiled=True)  6.28 us
    unnamed x36, local copies, waits for them, and re-layouts  6.23 us
    dot_general x1, matrix products, on_device(): jnp.einsum('pkj,kps->jps', weight_stack, state_full, preferred_element_ty...  5.09 us
  transfers between devices with their start and end apart: 4, of which 4 were waited for; matrix products, arithmetic and copies ran while one was open for 13% of the time, Pallas kernels for 0%

profile of v1, /device:TPU:32, one launch (start us, length us, event | category | flops | bytes accessed | tf_op | source)
XLA Modules:
  0.0 193.7 jit_solution(11152632563793393357)
XLA Ops:
  0.0 1.0 pad_maximum_fusion.1
  1.0 3.1 %collective-permute-start.1 = (bf16[34,4,4,128]{3,2,1,0:T(4,128)(2,1)S(1)}, bf16[34,4,4,128]{3,2,1,0:T(4,128)(2,1)S(1)}, u32[]{:S(2)}, u32[]{:S(2)}) collective-permute-start(bf16[34,4,4,128]{3,2,1,0:T(4,128)(2,1)S(1)} %pad_maximum_fusion.1), channel_id=1, source_target_pairs={{2,0},{4,2},{6,4},{0,6},{3,1},{5,3},{7,5},{1,7},{10,8},{12,10},{14... | collective-permute-start | bytes 417800 | tf_op jit(solution)/shard_map/ppermute | solution.py:28
  4.1 0.0 collective-permute-start
  4.1 0.7 compare_select_fusion
  4.8 0.1 copy.16
  4.9 0.1 reshape.104
  5.0 2.0 %collective-permute-done.1 = bf16[34,4,4,128]{3,2,1,0:T(4,128)(2,1)S(1)} collective-permute-done((bf16[34,4,4,128]{3,2,1,0:T(4,128)(2,1)S(1)}, bf16[34,4,4,128]{3,2,1,0:T(4,128)(2,1)S(1)}, u32[]{:S(2)}, u32[]{:S(2)}) %collective-permute-start.1) | collective-permute-done | bytes 139296 | tf_op jit(solution)/shard_map/ppermute | solution.py:28
  7.1 3.4 %collective-permute-done = bf16[34,4,4,128]{3,2,1,0:T(4,128)(2,1)S(1)} collective-permute-done((bf16[34,4,4,128]{3,2,1,0:T(4,128)(2,1)S(1)}, bf16[34,4,4,128]{3,2,1,0:T(4,128)(2,1)S(1)}, u32[]{:S(2)}, u32[]{:S(2)}) %collective-permute-start) | collective-permute-done | bytes 139296 | tf_op jit(solution)/shard_map/ppermute | solution.py:25
  10.5 1.2 pad_maximum_fusion
  11.7 0.3 copy.15
  12.0 0.8 gather_fusion
  12.8 0.6 copy.25
  13.4 0.6 slice.22
  14.1 0.4 reshape.117
  14.5 1.6 copy.21
  16.1 11.2 %all-to-all-start = ((bf16[32,32,512]{2,0,1:T(8,128)(2,1)}), bf16[32,32,512]{2,0,1:T(8,128)(2,1)S(1)}, u32[]{:S(2)}, u32[]{:S(2)}) async-start(bf16[32,32,512]{2,0,1:T(8,128)(2,1)} %copy.21), calls=%async_computation | async-start | bytes 2097152 | tf_op jit(solution)/shard_map/all_to_all | solution.py:87
  27.3 4.7 %copy.24 = bf16[32,32,1,1280]{3,0,1,2:T(8,128)(2,1)} copy(bf16[32,32,1,1280]{3,1,2,0:T(8,128)(2,1)} %param.13) | data formatting | bytes 5242880 | tf_op args[6]
  31.9 21.7 %all-to-all-done = bf16[32,32,512]{2,0,1:T(8,128)(2,1)S(1)} async-done(((bf16[32,32,512]{2,0,1:T(8,128)(2,1)}), bf16[32,32,512]{2,0,1:T(8,128)(2,1)S(1)}, u32[]{:S(2)}, u32[]{:S(2)}) %all-to-all-start) | async-done | bytes 1048608 | tf_op jit(solution)/shard_map/all_to_all | solution.py:87
  53.6 0.0 copy-start.1
  53.6 6.3 %all-to-all-start.1 = ((bf16[32,32,1280]{2,0,1:T(8,128)(2,1)}), bf16[32,32,1280]{2,0,1:T(8,128)(2,1)}, u32[]{:S(2)}, u32[]{:S(2)}) async-start(bf16[32,32,1280]{2,0,1:T(8,128)(2,1)} %bitcast.185), calls=%async_computation.1 | async-start | bytes 5242880 | tf_op jit(solution)/shard_map/all_to_all | solution.py:105
  60.6 0.0 copy-done.1
  60.6 0.1 convert_multiply_fusion
  60.7 0.2 multiply_convert_fusion
  60.9 0.4 fusion.64
  61.3 3.9 %select_reduce_fusion = (f32[]{:T(128)}, f32[1024,1024]{1,0:T(8,128)}) fusion(bf16[1024,512]{1,0:T(8,128)(2,1)S(1)} %bitcast.195, bf16[1024,512]{1,0:T(8,128)(2,1)S(1)} %bitcast.193), kind=kOutput, calls=%fused_computation.10 | convolution fusion | flops 1080033280 | bytes 6291460 | tf_op jit(solution)/shard_map/while/body/eval_jaxpr/dot_general | solution.py:95
  65.9 2.8 %divide_convert_fusion.1 = bf16[1024,1024]{1,0:T(8,128)(2,1)S(1)} fusion(f32[1024,1024]{1,0:T(8,128)} %get-tuple-element.16, f32[]{:T(128)S(6)} %div.29), kind=kLoop, calls=%fused_computation.9 | loop fusion | flops 6291456 | bytes 6291460 | tf_op jit(solution)/shard_map/while/body/eval_jaxpr/convert_element_type | solution.py:60
  68.7 0.0 copy-start
  68.7 1.3 copy-done
  70.0 3.7 %fusion.21 = bf16[1024,1024]{1,0:T(8,128)(2,1)} fusion(bf16[1024,1024]{1,0:T(8,128)(2,1)S(1)} %divide_convert_fusion.1), kind=kOutput, calls=%fused_computation.24 | convolution fusion | flops 2153775104 | bytes 4194304 | tf_op jit(solution)/shard_map/while/body/eval_jaxpr/dot_general | solution.py:47
  73.8 7.4 %divide_convert_fusion = bf16[1024,1024]{1,0:T(8,128)(2,1)S(1)} fusion(f32[]{:T(128)S(6)} %sqrt.4, bf16[1024,1024]{1,0:T(8,128)(2,1)} %fusion.21, bf16[1024,1024]{1,0:T(8,128)(2,1)} %copy-done), kind=kOutput, calls=%fused_computation.8 | convolution fusion | flops 4314890240 | bytes 6291460 | tf_op jit(solution)/shard_map/while/body/eval_jaxpr/dot_general | solution.py:46
  81.1 0.6 fusion.65
  81.8 0.6 fusion.66
  82.4 36.8 %all-to-all-done.1 = bf16[32,32,1280]{2,0,1:T(8,128)(2,1)} async-done(((bf16[32,32,1280]{2,0,1:T(8,128)(2,1)}), bf16[32,32,1280]{2,0,1:T(8,128)(2,1)}, u32[]{:S(2)}, u32[]{:S(2)}) %all-to-all-start.1) | async-done | bytes 2621472 | tf_op jit(solution)/shard_map/all_to_all | solution.py:105
  119.3 5.1 %fusion.4 = bf16[1024,1,1280]{2,0,1:T(8,128)(2,1)S(1)} fusion(bf16[1024,1280]{1,0:T(8,128)(2,1)} %bitcast.22, bf16[1024,1024]{1,0:T(8,128)(2,1)S(1)} %divide_convert_fusion, f32[1024]{0:T(1024)S(1)} %bitcast.202), kind=kOutput, calls=%fused_computation.14 | convolution fusion | flops 2688811008 | bytes 7344128 | tf_op jit(solution)/shard_map/pkj,kps->jps/dot_general | solution.py:106
  124.9 65.9 %all_to_all.35 = bf16[32,32,1,1280]{3,1,2,0:T(8,128)(2,1)S(1)} all-to-all(bf16[32,32,1,1280]{3,1,2,0:T(8,128)(2,1)S(1)} %fusion.23), channel_id=1, replica_groups=mesh['mem'=32,'lon'=4,'lat'=2] {'mem'}, dimensions={0} | all-to-all | bytes 5242880 | tf_op jit(solution)/shard_map/all_to_all | solution.py:12
  190.8 2.9 %copy.20 = bf16[32,32,1,1280]{3,1,2,0:T(8,128)(2,1)} copy(bf16[32,32,1,1280]{3,0,2,1:T(8,128)(2,1)S(1)} %bitcast.188) | data formatting | bytes 5242880 | tf_op jit(solution)/shard_map/reshape | solution.py:13
  (41 shorter events, 0.3 us)
Async XLA Ops:
  1.0 6.0 %collective-permute-start.1 = (bf16[34,4,4,128]{3,2,1,0:T(4,128)(2,1)S(1)}, bf16[34,4,4,128]{3,2,1,0:T(4,128)(2,1)S(1)}, u32[]{:S(2)}, u32[]{:S(2)}) collective-permute-start(bf16[34,4,4,128]{3,2,1,0:T(4,128)(2,1)S(1)} %pad_maximum_fusion.1), channel_id=1, source_target_pairs={{2,0},{4,2},{6,4},{0,6},{3,1},{5,3},{7,5},{1,7},{10,8},{12,10},{14... | collective-permute-start | bytes 417800 | tf_op jit(solution)/shard_map/ppermute | solution.py:28
  4.1 6.3 %collective-permute-start = (bf16[34,4,4,128]{3,2,1,0:T(4,128)(2,1)S(1)}, bf16[34,4,4,128]{3,2,1,0:T(4,128)(2,1)S(1)}, u32[]{:S(2)}, u32[]{:S(2)}) collective-permute-start(bf16[34,4,4,128]{3,2,1,0:T(4,128)(2,1)S(1)} %pad_maximum_fusion.1), channel_id=1, source_target_pairs={{0,2},{2,4},{4,6},{6,0},{1,3},{3,5},{5,7},{7,1},{8,10},{10,12},{12... | collective-permute-start | bytes 417800 | tf_op jit(solution)/shard_map/ppermute | solution.py:25
  16.1 37.6 %all-to-all-start = ((bf16[32,32,512]{2,0,1:T(8,128)(2,1)}), bf16[32,32,512]{2,0,1:T(8,128)(2,1)S(1)}, u32[]{:S(2)}, u32[]{:S(2)}) async-start(bf16[32,32,512]{2,0,1:T(8,128)(2,1)} %copy.21), calls=%async_computation | async-start | bytes 2097152 | tf_op jit(solution)/shard_map/all_to_all | solution.py:87
  53.6 6.9 %copy-start.1 = (f32[1,1,4]{2,1,0:T(1,128)S(1)}, f32[1,1,4]{2,1,0:T(1,128)}, u32[]{:S(2)}) copy-start(f32[1,1,4]{2,1,0:T(1,128)} %param.12) | copy-start | bytes 52
  53.6 65.7 %all-to-all-start.1 = ((bf16[32,32,1280]{2,0,1:T(8,128)(2,1)}), bf16[32,32,1280]{2,0,1:T(8,128)(2,1)}, u32[]{:S(2)}, u32[]{:S(2)}) async-start(bf16[32,32,1280]{2,0,1:T(8,128)(2,1)} %bitcast.185), calls=%async_computation.1 | async-start | bytes 5242880 | tf_op jit(solution)/shard_map/all_to_all | solution.py:105
  68.7 1.3 copy-start
